TPU v7x, 32 devices: a whole 2x2x4 slice. The times are simulated.
32 devices in a mesh: runs: 2 (over x), tm: 16 (over z, y, core), pix: 1.
Axes of the slice: x: 2, y: 2, z: 4, core: 2. Of those that a mesh axis runs over, the one named last changes fastest.
Arguments:
- intensity: float32 [2048, 4096], P('tm', ('runs', 'pix')), parts along dimension 1, may hold values from 0.01 to 60
- cycle_label: int32 [4096], P(('runs', 'pix')), parts along dimension 0, may hold values from 0 to 127, as said below
- valid_mask: int32 [4096], P(('runs', 'pix')), parts along dimension 0, may hold values from 0 to 1, as said below
Outputs:
- correlation: float32 [128, 4096], P('tm', ('runs', 'pix')), parts along dimension 1
There are 2 independent parts, one for each index of `runs`. A program takes and returns all parts, laid end to end along the dimension named above; each array names one. Nothing has to cross between parts.
Inputs may be any that keep to these rules, and one draw needn't show every extreme that they name: `cycle_label`: every cycle 0 to 127 is the label of exactly 16 pixels. `valid_mask`: every cycle holds at least one pixel marked 1.
All inputs are finite; a program needn't handle non-finite values.
Results may differ from a plain program's by a relative error of at most 0.0001.
Values sent between devices are 32-bit elements; how exact they have to be, the bound alone decides.
A program may use at most 64 MiB of HBM per device.

v0:
```python
import jax
import jax.numpy as jnp
from jax import lax
from jax.sharding import PartitionSpec as P

Q = 128
LEVELS = 8
LAGS = 16


def coarsen(series):
    paired = series.reshape(series.shape[0] // 2, 2, series.shape[1])
    return (paired[:, 0] + paired[:, 1]) * 0.5


def level_rows(series, extension, total_frames):
    frames_here = series.shape[0]
    row_list = []
    for offset in range(extension.shape[0] + 1):
        inside = min(offset, frames_here)
        total = jnp.sum(series[: frames_here - inside] * series[inside:], axis=0)
        if offset > 0:
            tail_rows = series[frames_here - inside :]
            total = total + jnp.sum(tail_rows * extension[offset - inside : offset], axis=0)
        row_list.append(total / (total_frames - offset))
    return row_list


def pixel_rows(gathered):
    series = gathered[:, 0, :]
    row_list = []
    for height in range(LEVELS):
        if height > 0:
            series = coarsen(series)
        extension = jnp.zeros((LAGS - 1, series.shape[1]), jnp.float32)
        row_list = row_list + level_rows(series, extension, series.shape[0])
    return jnp.stack(row_list)


def body(intensity, cycle_label, valid_mask):
    valid_flag = valid_mask.astype(jnp.float32)
    member = (cycle_label[:, None] == jnp.arange(Q, dtype=jnp.int32)[None, :]).astype(jnp.float32)
    weighted = member * valid_flag[:, None]
    partial_sum = jnp.dot(intensity, weighted, precision=lax.Precision.HIGHEST)
    partial_count = jnp.sum(weighted, axis=0)
    cycle_sum, cycle_count = lax.psum((partial_sum, partial_count), "pix")
    cycle_mean = cycle_sum / cycle_count[None, :]
    per_pixel = lax.dot_general(
        cycle_mean, member, (((1,), (1,)), ((), ())), precision=lax.Precision.HIGHEST
    )
    normed = valid_flag[None, :] * intensity / per_pixel
    devices_tm = lax.axis_size("tm")
    tile_width = normed.shape[1] // devices_tm
    pieces = normed.reshape(normed.shape[0], devices_tm, tile_width)
    rows_local = pixel_rows(lax.all_to_all(pieces, "tm", split_axis=1, concat_axis=0, tiled=True))
    return lax.all_to_all(rows_local, "tm", split_axis=0, concat_axis=1, tiled=True)


def solution(mesh):
    placed = (P("tm", ("runs", "pix")), P(("runs", "pix")), P(("runs", "pix")))
    return jax.shard_map(
        body, mesh=mesh, in_specs=placed, out_specs=P("tm", ("runs", "pix")), check_vma=False
    )
```

profile of v0, /device:TPU:0, one launch (start us, length us, event | category | flops | bytes accessed | tf_op | source)
XLA Modules:
  0.0 95.0 jit_solution(12186441031817750926)
XLA Ops:
  0.0 0.8 convert_element_type.4
  0.8 0.7 select_reduce_fusion
  1.5 3.6 %fusion.3 = f32[128,128]{1,0:T(8,128)S(1)} fusion(f32[128,2048]{1,0:T(8,128)} %param.3, f32[2048]{0:T(1024)S(1)} %convert_element_type.4, s32[2048]{0:T(1024)S(1)} %copy-done, f32[128]{0:T(128)S(1)} %select_reduce_fusion), kind=kOutput, calls=%fused_computation.5 | convolution fusion | flops 403193856 | bytes 1131008 | tf_op jit(solution)/shard_map/dot_general | solution.py:44
  5.1 1.2 %fusion.2 = f32[16,16,8,128]{3,2,1,0:T(8,128)S(1)} fusion(f32[128,128]{1,0:T(8,128)S(1)} %fusion.3, f32[128,2048]{1,0:T(8,128)S(1)} %copy-done.1, s32[2048]{0:T(1024)S(1)} %copy-done, f32[2048]{0:T(1024)S(1)} %convert_element_type.4), kind=kOutput, calls=%fused_computation.4 | convolution fusion | flops 403439616 | bytes 2179072 | tf_op jit(solution)/shard_map/dot_general | solution.py:48
  6.5 31.9 %all_to_all.34 = f32[128,16,128]{2,0,1:T(8,128)S(1)} all-to-all(f32[128,16,128]{2,0,1:T(8,128)S(1)} %bitcast.378), channel_id=1, replica_groups=mesh['runs'=2,'tm'=16,'pix'=1] {'tm'}, dimensions={1} | all-to-all | bytes 2097152 | tf_op jit(solution)/shard_map/all_to_all | solution.py:55
  43.0 1.2 %multiply_reduce_fusion = (f32[128]{0:T(128)S(1)}, f32[1024,1,128]{2,1,0:T(1,128)S(1)}) fusion(f32[1024,2,128]{2,1,0:T(2,128)S(1)} %bitcast.370), kind=kLoop, calls=%fused_computation.42 | loop fusion | flops 524160 | bytes 1573376 | tf_op jit(solution)/shard_map/reduce_sum | solution.py:21
  44.2 1.1 %fusion.36 = f32[128]{0:T(128)S(1)} fusion(f32[1024,1,128]{2,1,0:T(1,128)S(1)} %get-tuple-element.46), kind=kLoop, calls=%fused_computation.66 | loop fusion | flops 259456 | bytes 1038848 | tf_op jit(solution)/shard_map/reduce_sum | solution.py:21
  45.3 1.1 %fusion.38 = f32[128]{0:T(128)S(1)} fusion(f32[1024,1,128]{2,1,0:T(1,128)S(1)} %get-tuple-element.46), kind=kLoop, calls=%fused_computation.70 | loop fusion | flops 258944 | bytes 1036800 | tf_op jit(solution)/shard_map/reduce_sum | solution.py:21
  46.4 1.1 %fusion.35 = f32[128]{0:T(128)S(1)} fusion(f32[1024,1,128]{2,1,0:T(1,128)S(1)} %get-tuple-element.46), kind=kLoop, calls=%fused_computation.64 | loop fusion | flops 259712 | bytes 1039872 | tf_op jit(solution)/shard_map/reduce_sum | solution.py:21
  47.5 1.1 %fusion.39 = f32[128]{0:T(128)S(1)} fusion(f32[1024,1,128]{2,1,0:T(1,128)S(1)} %get-tuple-element.46), kind=kLoop, calls=%fused_computation.72 | loop fusion | flops 258688 | bytes 1035776 | tf_op jit(solution)/shard_map/reduce_sum | solution.py:21
  48.6 1.1 %fusion.34 = f32[128]{0:T(128)S(1)} fusion(f32[1024,1,128]{2,1,0:T(1,128)S(1)} %get-tuple-element.46), kind=kLoop, calls=%fused_computation.62 | loop fusion | flops 259968 | bytes 1040896 | tf_op jit(solution)/shard_map/reduce_sum | solution.py:21
  49.8 1.1 %fusion.33 = f32[128]{0:T(128)S(1)} fusion(f32[1024,1,128]{2,1,0:T(1,128)S(1)} %get-tuple-element.46), kind=kLoop, calls=%fused_computation.60 | loop fusion | flops 260224 | bytes 1041920 | tf_op jit(solution)/shard_map/reduce_sum | solution.py:21
  50.9 1.1 %fusion.32 = f32[128]{0:T(128)S(1)} fusion(f32[1024,1,128]{2,1,0:T(1,128)S(1)} %get-tuple-element.46), kind=kLoop, calls=%fused_computation.58 | loop fusion | flops 260480 | bytes 1042944 | tf_op jit(solution)/shard_map/reduce_sum | solution.py:21
  52.0 1.1 %fusion.40 = f32[128]{0:T(128)S(1)} fusion(f32[1024,1,128]{2,1,0:T(1,128)S(1)} %get-tuple-element.46), kind=kLoop, calls=%fused_computation.74 | loop fusion | flops 258432 | bytes 1034752 | tf_op jit(solution)/shard_map/reduce_sum | solution.py:21
  53.1 1.1 %fusion.31 = f32[128]{0:T(128)S(1)} fusion(f32[1024,1,128]{2,1,0:T(1,128)S(1)} %get-tuple-element.46), kind=kLoop, calls=%fused_computation.56 | loop fusion | flops 260736 | bytes 1043968 | tf_op jit(solution)/shard_map/reduce_sum | solution.py:21
  54.2 1.1 %fusion.30 = f32[128]{0:T(128)S(1)} fusion(f32[1024,1,128]{2,1,0:T(1,128)S(1)} %get-tuple-element.46), kind=kLoop, calls=%fused_computation.54 | loop fusion | flops 260992 | bytes 1044992 | tf_op jit(solution)/shard_map/reduce_sum | solution.py:21
  55.3 1.3 %fusion.37 = f32[128]{0:T(128)S(1)} fusion(f32[1024,1,128]{2,1,0:T(1,128)S(1)} %get-tuple-element.46), kind=kLoop, calls=%fused_computation.68 | loop fusion | flops 259200 | bytes 1037824 | tf_op jit(solution)/shard_map/reduce_sum | solution.py:21
  56.6 1.1 %fusion.29 = f32[128]{0:T(128)S(1)} fusion(f32[1024,1,128]{2,1,0:T(1,128)S(1)} %get-tuple-element.46), kind=kLoop, calls=%fused_computation.52 | loop fusion | flops 261248 | bytes 1046016 | tf_op jit(solution)/shard_map/reduce_sum | solution.py:21
  57.7 1.1 %fusion.41 = f32[128]{0:T(128)S(1)} fusion(f32[1024,1,128]{2,1,0:T(1,128)S(1)} %get-tuple-element.46), kind=kLoop, calls=%fused_computation.76 | loop fusion | flops 258176 | bytes 1033728 | tf_op jit(solution)/shard_map/reduce_sum | solution.py:21
  58.8 1.1 %fusion.28 = f32[128]{0:T(128)S(1)} fusion(f32[1024,1,128]{2,1,0:T(1,128)S(1)} %get-tuple-element.46), kind=kLoop, calls=%fused_computation.50 | loop fusion | flops 261504 | bytes 1047040 | tf_op jit(solution)/shard_map/reduce_sum | solution.py:21
  60.0 1.1 %fusion.27 = f32[128]{0:T(128)S(1)} fusion(f32[1024,1,128]{2,1,0:T(1,128)S(1)} %get-tuple-element.46), kind=kLoop, calls=%fused_computation.48 | loop fusion | flops 261760 | bytes 1048064 | tf_op jit(solution)/shard_map/reduce_sum | solution.py:21
  61.1 0.6 multiply_reduce_fusion.1
  63.9 0.5 fusion.50
  64.5 0.5 fusion.49
  65.1 0.5 fusion.48
  66.2 0.6 fusion.47
  66.9 0.6 fusion.46
  68.0 0.6 fusion.45
  69.1 0.6 fusion.44
  69.7 0.6 fusion.43
  82.6 11.7 %all_to_all.35 = f32[16,8,128]{2,1,0:T(8,128)S(1)} all-to-all(f32[16,8,128]{2,1,0:T(8,128)S(1)} %bitcast.379), channel_id=1, replica_groups=mesh['runs'=2,'tm'=16,'pix'=1] {'tm'}, dimensions={0} | all-to-all | bytes 131072 | tf_op jit(solution)/shard_map/all_to_all | solution.py:56
  94.4 0.6 copy.12
  (270 shorter events, 21.1 us)
Async XLA Ops:
  0.0 0.8 copy-start
  0.0 5.1 %copy-start.1 = (f32[128,2048]{1,0:T(8,128)S(1)}, f32[128,2048]{1,0:T(8,128)}, u32[]{:S(2)}) copy-start(f32[128,2048]{1,0:T(8,128)} %param.3) | copy-start | bytes 3145732
where the time goes:
time: 95.3 us; the launch traced here: 95 us
  other arithmetic  44.8 us (47%)
  blocking collectives  43.6 us (46%)
  matrix products  4.86 us (5%)
  local copies, waits for them, and re-layouts  1.1 us (1%)
    reduce_sum x119, other arithmetic, level_rows(): total = jnp.sum(series[:frames_here - inside] * series[inside:], axis=0)  40.1 us
    all_to_all x1, blocking collectives, body(): lax.all_to_all(pieces, 'tm', split_axis=1, concat_axis=0, tiled=True)  31.9 us
    all_to_all x1, blocking collectives, body(): lax.all_to_all(rows_local, 'tm', split_axis=0, concat_axis=1, tiled=True)  11.7 us
    dot_general x1, matrix products, body(): partial_sum = jnp.dot(intensity, weighted, precision=lax.Precision.HIGHEST)  3.63 us
    reduce_sum x106, other arithmetic, level_rows(): jnp.sum(tail_rows * extension[offset - inside:offset], axis=0)  2.74 us

commit v1 on v0

--- a/solution.py
+++ b/solution.py
@@ -6,6 +6,28 @@
 Q = 128
 LEVELS = 8
 LAGS = 16
+
+
+def cut_along(x, dim, length):
+    before, after = (x.shape[:dim], x.shape[dim + 1 :])
+    return jnp.moveaxis(x.reshape(*before, length, -1, *after), dim, 0)
+
+
+def laid_out(tiles, dim):
+    tiles = jnp.moveaxis(tiles, 0, dim)
+    dims = tiles.shape
+    return tiles.reshape(*dims[:dim], dims[dim] * dims[dim + 1], *dims[dim + 2 :])
+
+
+def exchange_directly(x, axis, split_dim, concat_dim):
+    size, mine = (lax.axis_size(axis), lax.axis_index(axis))
+    blocks = cut_along(x, split_dim, size)
+    outs = [blocks[mine]]
+    for step in range(1, size):
+        sent = blocks[(mine + step) % size]
+        outs.append(lax.ppermute(sent, axis, [(i, (i + step) % size) for i in range(size)]))
+    blocks = jnp.stack(outs)[(mine - jnp.arange(size)) % size]
+    return laid_out(blocks, concat_dim)
 
 
 def coarsen(series):
@@ -52,7 +74,7 @@
     devices_tm = lax.axis_size("tm")
     tile_width = normed.shape[1] // devices_tm
     pieces = normed.reshape(normed.shape[0], devices_tm, tile_width)
-    rows_local = pixel_rows(lax.all_to_all(pieces, "tm", split_axis=1, concat_axis=0, tiled=True))
+    rows_local = pixel_rows(exchange_directly(pieces, "tm", 1, 0))
     return lax.all_to_all(rows_local, "tm", split_axis=0, concat_axis=1, tiled=True)
 
 

time: 95.3 us -> 98.4 us (1.033)
  blocking collectives: 43.6 us -> 12.7 us
  starting transfers between devices: 0 us -> 21.9 us
  waiting for transfers between devices: 0 us -> 9.47 us
  local copies, waits for them, and re-layouts: 1.1 us -> 4.27 us
    all_to_all x1 -> x0, blocking collectives: 31.9 us -> none  [body(): lax.all_to_all(pieces, 'tm', split_axis=1, concat_axis=0, tiled=True)]
    ppermute x0 -> x15, starting transfers between devices: none -> 21.9 us  [exchange_directly(): lax.ppermute(sent, axis, [(i, (i + step) % size) for i in range(size)])]
    ppermute x0 -> x15, waiting for transfers between devices: none -> 9.47 us  [exchange_directly(): lax.ppermute(sent, axis, [(i, (i + step) % size) for i in range(size)])]
    unnamed x5 -> x23, local copies, waits for them, and re-layouts: 0.64 us -> 2.3 us
    another operation x0 -> x2, local copies, waits for them, and re-layouts: none -> 0.99 us
  transfers between devices with their start and end apart: 0 -> 15, of which waited for: 0 -> 5; matrix products, arithmetic and copies ran while one was open for 0% -> 0% of each run, Pallas kernels for 0% -> 0%
where the time goes in v1:
time: 98.4 us; the launch traced here: 98.1 us
  other arithmetic  44.1 us (45%)
  starting transfers between devices  21.9 us (22%)
  blocking collectives  12.7 us (13%)
  waiting for transfers between devices  9.47 us (10%)
  matrix products  4.88 us (5%)
  local copies, waits for them, and re-layouts  4.27 us (4%)
    reduce_sum x119, other arithmetic, level_rows(): total = jnp.sum(series[:frames_here - inside] * series[inside:], axis=0)  40.1 us
    ppermute x15, starting transfers between devices, exchange_directly(): lax.ppermute(sent, axis, [(i, (i + step) % size) for i in range(size)])  21.9 us
    all_to_all x1, blocking collectives, body(): lax.all_to_all(rows_local, 'tm', split_axis=0, concat_axis=1, tiled=True)  12.7 us
    ppermute x15, waiting for transfers between devices, exchange_directly(): lax.ppermute(sent, axis, [(i, (i + step) % size) for i in range(size)])  9.47 us
    dot_general x1, matrix products, body(): partial_sum = jnp.dot(intensity, weighted, precision=lax.Precision.HIGHEST)  3.63 us
    reduce_sum x106, other arithmetic, level_rows(): jnp.sum(tail_rows * extension[offset - inside:offset], axis=0)  2.74 us
    unnamed x23, local copies, waits for them, and re-layouts  2.3 us
  transfers between devices with their start and end apart: 15, of which 5 were waited for; matrix products, arithmetic and copies ran while one was open for 0% of the time, Pallas kernels for 0%

profile of v1, /device:TPU:0, one launch (start us, length us, event | category | flops | bytes accessed | tf_op | source)
XLA Modules:
  0.0 98.1 jit_solution(9811610050498867715)
XLA Ops:
  1.4 0.7 select_reduce_fusion
  2.1 3.6 %fusion.3 = f32[128,128]{1,0:T(8,128)S(1)} fusion(f32[128,2048]{1,0:T(8,128)} %param.3, f32[2048]{0:T(1024)S(1)} %convert_element_type.4, s32[2048]{0:T(1024)S(1)} %copy-done.1, f32[128]{0:T(128)S(1)} %select_reduce_fusion), kind=kOutput, calls=%fused_computation.6 | convolution fusion | flops 403193856 | bytes 1131008 | tf_op jit(solution)/shard_map/dot_general | solution.py:66
  5.7 1.3 %fusion.2 = f32[16,8,16,128]{3,1,2,0:T(8,128)S(1)} fusion(f32[128,128]{1,0:T(8,128)S(1)} %fusion.3, f32[128,2048]{1,0:T(8,128)S(1)} %copy-done.2, s32[2048]{0:T(1024)S(1)} %copy-done.1, f32[2048]{0:T(1024)S(1)} %convert_element_type.4), kind=kOutput, calls=%fused_computation.5 | convolution fusion | flops 403439616 | bytes 2179072 | tf_op jit(solution)/shard_map/dot_general | solution.py:70
  7.3 1.0 %constant_dynamic-slice_fusion = (f32[128,1,1,128]{3,1,0,2:T(1,128)S(1)}, f32[128,1,1,128]{3,1,0,2:T(1,128)S(1)}, f32[128,1,1,128]{3,1,0,2:T(1,128)S(1)}, f32[12...) fusion(f32[128,16,1,128]{3,1,0,2:T(8,128)S(1)} %bitcast.419, ...), kind=kLoop, calls=%fused_computation.396 | loop fusion | bytes 2097216 | tf_op jit(solution)/shard_map/dynamic-slice.15
  8.8 2.6 %collective-permute-start.1 = (f32[128,1,128]{2,0,1:T(8,128)S(1)}, f32[128,1,128]{2,0,1:T(8,128)S(1)}, u32[]{:S(2)}, u32[]{:S(2)}) collective-permute-start(f32[128,1,128]{2,0,1:T(8,128)S(1)} %bitcast.437), channel_id=1, source_target_pairs={{0,2},{1,3},{2,4},{3,5},{4,6},{5,7},{6,8},{7,9},{8,10},{9,11},{10,... | collective-permute-start | bytes 196616 | tf_op jit(solution)/shard_map/ppermute | solution.py:28
  11.4 2.4 %collective-permute-start.2 = (f32[128,1,128]{2,0,1:T(8,128)S(1)}, f32[128,1,128]{2,0,1:T(8,128)S(1)}, u32[]{:S(2)}, u32[]{:S(2)}) collective-permute-start(f32[128,1,128]{2,0,1:T(8,128)S(1)} %bitcast.436), channel_id=1, source_target_pairs={{0,3},{1,4},{2,5},{3,6},{4,7},{5,8},{6,9},{7,10},{8,11},{9,12},{10... | collective-permute-start | bytes 196616 | tf_op jit(solution)/shard_map/ppermute | solution.py:28
  13.8 1.6 %collective-permute-start.3 = (f32[128,1,128]{2,0,1:T(8,128)S(1)}, f32[128,1,128]{2,0,1:T(8,128)S(1)}, u32[]{:S(2)}, u32[]{:S(2)}) collective-permute-start(f32[128,1,128]{2,0,1:T(8,128)S(1)} %bitcast.435), channel_id=1, source_target_pairs={{0,4},{1,5},{2,6},{3,7},{4,8},{5,9},{6,10},{7,11},{8,12},{9,13},{1... | collective-permute-start | bytes 196616 | tf_op jit(solution)/shard_map/ppermute | solution.py:28
  15.7 1.1 %collective-permute-start.5 = (f32[128,1,128]{2,0,1:T(8,128)S(1)}, f32[128,1,128]{2,0,1:T(8,128)S(1)}, u32[]{:S(2)}, u32[]{:S(2)}) collective-permute-start(f32[128,1,128]{2,0,1:T(8,128)S(1)} %bitcast.433), channel_id=1, source_target_pairs={{0,6},{1,7},{2,8},{3,9},{4,10},{5,11},{6,12},{7,13},{8,14},{9,15},... | collective-permute-start | bytes 196616 | tf_op jit(solution)/shard_map/ppermute | solution.py:28
  16.8 4.4 %collective-permute-start.6 = (f32[128,1,128]{2,0,1:T(8,128)S(1)}, f32[128,1,128]{2,0,1:T(8,128)S(1)}, u32[]{:S(2)}, u32[]{:S(2)}) collective-permute-start(f32[128,1,128]{2,0,1:T(8,128)S(1)} %bitcast.432), channel_id=1, source_target_pairs={{0,7},{1,8},{2,9},{3,10},{4,11},{5,12},{6,13},{7,14},{8,15},{9,0},... | collective-permute-start | bytes 196616 | tf_op jit(solution)/shard_map/ppermute | solution.py:28
  22.0 6.5 %collective-permute-done.4 = f32[128,1,128]{2,0,1:T(8,128)S(1)} collective-permute-done((f32[128,1,128]{2,0,1:T(8,128)S(1)}, f32[128,1,128]{2,0,1:T(8,128)S(1)}, u32[]{:S(2)}, u32[]{:S(2)}) %collective-permute-start.4) | collective-permute-done | bytes 65568 | tf_op jit(solution)/shard_map/ppermute | solution.py:28
  29.2 1.9 %collective-permute-start.11 = (f32[128,1,128]{2,0,1:T(8,128)S(1)}, f32[128,1,128]{2,0,1:T(8,128)S(1)}, u32[]{:S(2)}, u32[]{:S(2)}) collective-permute-start(f32[128,1,128]{2,0,1:T(8,128)S(1)} %bitcast.427), channel_id=1, source_target_pairs={{0,12},{1,13},{2,14},{3,15},{4,0},{5,1},{6,2},{7,3},{8,4},{9,5},{1... | collective-permute-start | bytes 196616 | tf_op jit(solution)/shard_map/ppermute | solution.py:28
  31.0 2.2 %collective-permute-start.12 = (f32[128,1,128]{2,0,1:T(8,128)S(1)}, f32[128,1,128]{2,0,1:T(8,128)S(1)}, u32[]{:S(2)}, u32[]{:S(2)}) collective-permute-start(f32[128,1,128]{2,0,1:T(8,128)S(1)} %bitcast.426), channel_id=1, source_target_pairs={{0,13},{1,14},{2,15},{3,0},{4,1},{5,2},{6,3},{7,4},{8,5},{9,6},{10... | collective-permute-start | bytes 196616 | tf_op jit(solution)/shard_map/ppermute | solution.py:28
  33.3 3.4 %collective-permute-start.13 = (f32[128,1,128]{2,0,1:T(8,128)S(1)}, f32[128,1,128]{2,0,1:T(8,128)S(1)}, u32[]{:S(2)}, u32[]{:S(2)}) collective-permute-start(f32[128,1,128]{2,0,1:T(8,128)S(1)} %bitcast.425), channel_id=1, source_target_pairs={{0,14},{1,15},{2,0},{3,1},{4,2},{5,3},{6,4},{7,5},{8,6},{9,7},{10,... | collective-permute-start | bytes 196616 | tf_op jit(solution)/shard_map/ppermute | solution.py:28
  37.3 2.1 %collective-permute-done.13 = f32[128,1,128]{2,0,1:T(8,128)S(1)} collective-permute-done((f32[128,1,128]{2,0,1:T(8,128)S(1)}, f32[128,1,128]{2,0,1:T(8,128)S(1)}, u32[]{:S(2)}, u32[]{:S(2)}) %collective-permute-start.13) | collective-permute-done | bytes 65568 | tf_op jit(solution)/shard_map/ppermute | solution.py:28
  40.5 1.2 %multiply_reduce_fusion.1 = (f32[128]{0:T(128)S(1)}, f32[1024,1,128]{2,1,0:T(1,128)S(1)}) fusion(f32[1024,2,128]{2,1,0:T(2,128)S(1)} %bitcast.382), kind=kLoop, calls=%fused_computation.41 | loop fusion | flops 524160 | bytes 1573376 | tf_op jit(solution)/shard_map/reduce_sum | solution.py:43
  58.1 0.8 fusion.48
  61.2 1.1 %fusion.40 = f32[128]{0:T(128)S(1)} fusion(f32[1024,1,128]{2,1,0:T(1,128)S(1)} %get-tuple-element.46), kind=kLoop, calls=%fused_computation.75 | loop fusion | flops 258176 | bytes 1033728 | tf_op jit(solution)/shard_map/reduce_sum | solution.py:43
  62.3 1.1 %fusion.38 = f32[128]{0:T(128)S(1)} fusion(f32[1024,1,128]{2,1,0:T(1,128)S(1)} %get-tuple-element.46), kind=kLoop, calls=%fused_computation.71 | loop fusion | flops 258688 | bytes 1035776 | tf_op jit(solution)/shard_map/reduce_sum | solution.py:43
  63.4 1.1 %fusion.39 = f32[128]{0:T(128)S(1)} fusion(f32[1024,1,128]{2,1,0:T(1,128)S(1)} %get-tuple-element.46), kind=kLoop, calls=%fused_computation.73 | loop fusion | flops 258432 | bytes 1034752 | tf_op jit(solution)/shard_map/reduce_sum | solution.py:43
  64.5 1.1 %fusion.36 = f32[128]{0:T(128)S(1)} fusion(f32[1024,1,128]{2,1,0:T(1,128)S(1)} %get-tuple-element.46), kind=kLoop, calls=%fused_computation.67 | loop fusion | flops 259200 | bytes 1037824 | tf_op jit(solution)/shard_map/reduce_sum | solution.py:43
  65.6 1.1 %fusion.37 = f32[128]{0:T(128)S(1)} fusion(f32[1024,1,128]{2,1,0:T(1,128)S(1)} %get-tuple-element.46), kind=kLoop, calls=%fused_computation.69 | loop fusion | flops 258944 | bytes 1036800 | tf_op jit(solution)/shard_map/reduce_sum | solution.py:43
  66.8 1.1 %fusion.34 = f32[128]{0:T(128)S(1)} fusion(f32[1024,1,128]{2,1,0:T(1,128)S(1)} %get-tuple-element.46), kind=kLoop, calls=%fused_computation.63 | loop fusion | flops 259712 | bytes 1039872 | tf_op jit(solution)/shard_map/reduce_sum | solution.py:43
  67.8 1.1 %fusion.35 = f32[128]{0:T(128)S(1)} fusion(f32[1024,1,128]{2,1,0:T(1,128)S(1)} %get-tuple-element.46), kind=kLoop, calls=%fused_computation.65 | loop fusion | flops 259456 | bytes 1038848 | tf_op jit(solution)/shard_map/reduce_sum | solution.py:43
  69.0 1.1 %fusion.32 = f32[128]{0:T(128)S(1)} fusion(f32[1024,1,128]{2,1,0:T(1,128)S(1)} %get-tuple-element.46), kind=kLoop, calls=%fused_computation.59 | loop fusion | flops 260224 | bytes 1041920 | tf_op jit(solution)/shard_map/reduce_sum | solution.py:43
  70.1 1.1 %fusion.33 = f32[128]{0:T(128)S(1)} fusion(f32[1024,1,128]{2,1,0:T(1,128)S(1)} %get-tuple-element.46), kind=kLoop, calls=%fused_computation.61 | loop fusion | flops 259968 | bytes 1040896 | tf_op jit(solution)/shard_map/reduce_sum | solution.py:43
  71.2 1.1 %fusion.30 = f32[128]{0:T(128)S(1)} fusion(f32[1024,1,128]{2,1,0:T(1,128)S(1)} %get-tuple-element.46), kind=kLoop, calls=%fused_computation.55 | loop fusion | flops 260736 | bytes 1043968 | tf_op jit(solution)/shard_map/reduce_sum | solution.py:43
  72.3 1.1 %fusion.31 = f32[128]{0:T(128)S(1)} fusion(f32[1024,1,128]{2,1,0:T(1,128)S(1)} %get-tuple-element.46), kind=kLoop, calls=%fused_computation.57 | loop fusion | flops 260480 | bytes 1042944 | tf_op jit(solution)/shard_map/reduce_sum | solution.py:43
  73.4 1.1 %fusion.28 = f32[128]{0:T(128)S(1)} fusion(f32[1024,1,128]{2,1,0:T(1,128)S(1)} %get-tuple-element.46), kind=kLoop, calls=%fused_computation.51 | loop fusion | flops 261248 | bytes 1046016 | tf_op jit(solution)/shard_map/reduce_sum | solution.py:43
  74.5 1.1 %fusion.29 = f32[128]{0:T(128)S(1)} fusion(f32[1024,1,128]{2,1,0:T(1,128)S(1)} %get-tuple-element.46), kind=kLoop, calls=%fused_computation.53 | loop fusion | flops 260992 | bytes 1044992 | tf_op jit(solution)/shard_map/reduce_sum | solution.py:43
  76.2 1.1 %fusion.26 = f32[128]{0:T(128)S(1)} fusion(f32[1024,1,128]{2,1,0:T(1,128)S(1)} %get-tuple-element.46), kind=kLoop, calls=%fused_computation.47 | loop fusion | flops 261760 | bytes 1048064 | tf_op jit(solution)/shard_map/reduce_sum | solution.py:43
  77.3 1.1 %fusion.27 = f32[128]{0:T(128)S(1)} fusion(f32[1024,1,128]{2,1,0:T(1,128)S(1)} %get-tuple-element.46), kind=kLoop, calls=%fused_computation.49 | loop fusion | flops 261504 | bytes 1047040 | tf_op jit(solution)/shard_map/reduce_sum | solution.py:43
  84.8 12.7 %all_to_all.19 = f32[16,8,128]{2,1,0:T(8,128)S(1)} all-to-all(f32[16,8,128]{2,1,0:T(8,128)S(1)} %bitcast.422), channel_id=1, replica_groups=mesh['runs'=2,'tm'=16,'pix'=1] {'tm'}, dimensions={0} | all-to-all | bytes 131072 | tf_op jit(solution)/shard_map/all_to_all | solution.py:78
  (321 shorter events, 31.7 us)
Async XLA Ops:
  0.0 0.7 copy-start
  0.7 0.7 copy-start.1
  0.7 5.0 %copy-start.2 = (f32[128,2048]{1,0:T(8,128)S(1)}, f32[128,2048]{1,0:T(8,128)}, u32[]{:S(2)}) copy-start(f32[128,2048]{1,0:T(8,128)} %param.3) | copy-start | bytes 3145732
  8.3 7.5 %collective-permute-start = (f32[128,1,128]{2,0,1:T(8,128)S(1)}, f32[128,1,128]{2,0,1:T(8,128)S(1)}, u32[]{:S(2)}, u32[]{:S(2)}) collective-permute-start(f32[128,1,128]{2,0,1:T(8,128)S(1)} %bitcast.438), channel_id=1, source_target_pairs={{0,1},{1,2},{2,3},{3,4},{4,5},{5,6},{6,7},{7,8},{8,9},{9,10},{10,1... | collective-permute-start | bytes 196616 | tf_op jit(solution)/shard_map/ppermute | solution.py:28
  8.8 8.0 %collective-permute-start.1 = (f32[128,1,128]{2,0,1:T(8,128)S(1)}, f32[128,1,128]{2,0,1:T(8,128)S(1)}, u32[]{:S(2)}, u32[]{:S(2)}) collective-permute-start(f32[128,1,128]{2,0,1:T(8,128)S(1)} %bitcast.437), channel_id=1, source_target_pairs={{0,2},{1,3},{2,4},{3,5},{4,6},{5,7},{6,8},{7,9},{8,10},{9,11},{10,... | collective-permute-start | bytes 196616 | tf_op jit(solution)/shard_map/ppermute | solution.py:28
  11.4 9.9 %collective-permute-start.2 = (f32[128,1,128]{2,0,1:T(8,128)S(1)}, f32[128,1,128]{2,0,1:T(8,128)S(1)}, u32[]{:S(2)}, u32[]{:S(2)}) collective-permute-start(f32[128,1,128]{2,0,1:T(8,128)S(1)} %bitcast.436), channel_id=1, source_target_pairs={{0,3},{1,4},{2,5},{3,6},{4,7},{5,8},{6,9},{7,10},{8,11},{9,12},{10... | collective-permute-start | bytes 196616 | tf_op jit(solution)/shard_map/ppermute | solution.py:28
  13.8 7.9 %collective-permute-start.3 = (f32[128,1,128]{2,0,1:T(8,128)S(1)}, f32[128,1,128]{2,0,1:T(8,128)S(1)}, u32[]{:S(2)}, u32[]{:S(2)}) collective-permute-start(f32[128,1,128]{2,0,1:T(8,128)S(1)} %bitcast.435), channel_id=1, source_target_pairs={{0,4},{1,5},{2,6},{3,7},{4,8},{5,9},{6,10},{7,11},{8,12},{9,13},{1... | collective-permute-start | bytes 196616 | tf_op jit(solution)/shard_map/ppermute | solution.py:28
  15.4 13.2 %collective-permute-start.4 = (f32[128,1,128]{2,0,1:T(8,128)S(1)}, f32[128,1,128]{2,0,1:T(8,128)S(1)}, u32[]{:S(2)}, u32[]{:S(2)}) collective-permute-start(f32[128,1,128]{2,0,1:T(8,128)S(1)} %bitcast.434), channel_id=1, source_target_pairs={{0,5},{1,6},{2,7},{3,8},{4,9},{5,10},{6,11},{7,12},{8,13},{9,14},{... | collective-permute-start | bytes 196616 | tf_op jit(solution)/shard_map/ppermute | solution.py:28
  15.7 13.0 %collective-permute-start.5 = (f32[128,1,128]{2,0,1:T(8,128)S(1)}, f32[128,1,128]{2,0,1:T(8,128)S(1)}, u32[]{:S(2)}, u32[]{:S(2)}) collective-permute-start(f32[128,1,128]{2,0,1:T(8,128)S(1)} %bitcast.433), channel_id=1, source_target_pairs={{0,6},{1,7},{2,8},{3,9},{4,10},{5,11},{6,12},{7,13},{8,14},{9,15},... | collective-permute-start | bytes 196616 | tf_op jit(solution)/shard_map/ppermute | solution.py:28
  16.8 12.3 %collective-permute-start.6 = (f32[128,1,128]{2,0,1:T(8,128)S(1)}, f32[128,1,128]{2,0,1:T(8,128)S(1)}, u32[]{:S(2)}, u32[]{:S(2)}) collective-permute-start(f32[128,1,128]{2,0,1:T(8,128)S(1)} %bitcast.432), channel_id=1, source_target_pairs={{0,7},{1,8},{2,9},{3,10},{4,11},{5,12},{6,13},{7,14},{8,15},{9,0},... | collective-permute-start | bytes 196616 | tf_op jit(solution)/shard_map/ppermute | solution.py:28
  21.2 9.8 %collective-permute-start.7 = (f32[128,1,128]{2,0,1:T(8,128)S(1)}, f32[128,1,128]{2,0,1:T(8,128)S(1)}, u32[]{:S(2)}, u32[]{:S(2)}) collective-permute-start(f32[128,1,128]{2,0,1:T(8,128)S(1)} %bitcast.431), channel_id=1, source_target_pairs={{0,8},{1,9},{2,10},{3,11},{4,12},{5,13},{6,14},{7,15},{8,0},{9,1},... | collective-permute-start | bytes 196616 | tf_op jit(solution)/shard_map/ppermute | solution.py:28
  21.6 11.6 %collective-permute-start.8 = (f32[128,1,128]{2,0,1:T(8,128)S(1)}, f32[128,1,128]{2,0,1:T(8,128)S(1)}, u32[]{:S(2)}, u32[]{:S(2)}) collective-permute-start(f32[128,1,128]{2,0,1:T(8,128)S(1)} %bitcast.430), channel_id=1, source_target_pairs={{0,9},{1,10},{2,11},{3,12},{4,13},{5,14},{6,15},{7,0},{8,1},{9,2},... | collective-permute-start | bytes 196616 | tf_op jit(solution)/shard_map/ppermute | solution.py:28
  28.5 8.1 %collective-permute-start.9 = (f32[128,1,128]{2,0,1:T(8,128)S(1)}, f32[128,1,128]{2,0,1:T(8,128)S(1)}, u32[]{:S(2)}, u32[]{:S(2)}) collective-permute-start(f32[128,1,128]{2,0,1:T(8,128)S(1)} %bitcast.429), channel_id=1, source_target_pairs={{0,10},{1,11},{2,12},{3,13},{4,14},{5,15},{6,0},{7,1},{8,2},{9,3},... | collective-permute-start | bytes 196616 | tf_op jit(solution)/shard_map/ppermute | solution.py:28
  28.7 8.5 %collective-permute-start.10 = (f32[128,1,128]{2,0,1:T(8,128)S(1)}, f32[128,1,128]{2,0,1:T(8,128)S(1)}, u32[]{:S(2)}, u32[]{:S(2)}) collective-permute-start(f32[128,1,128]{2,0,1:T(8,128)S(1)} %bitcast.428), channel_id=1, source_target_pairs={{0,11},{1,12},{2,13},{3,14},{4,15},{5,0},{6,1},{7,2},{8,3},{9,4},{... | collective-permute-start | bytes 196616 | tf_op jit(solution)/shard_map/ppermute | solution.py:28
  29.2 8.1 %collective-permute-start.11 = (f32[128,1,128]{2,0,1:T(8,128)S(1)}, f32[128,1,128]{2,0,1:T(8,128)S(1)}, u32[]{:S(2)}, u32[]{:S(2)}) collective-permute-start(f32[128,1,128]{2,0,1:T(8,128)S(1)} %bitcast.427), channel_id=1, source_target_pairs={{0,12},{1,13},{2,14},{3,15},{4,0},{5,1},{6,2},{7,3},{8,4},{9,5},{1... | collective-permute-start | bytes 196616 | tf_op jit(solution)/shard_map/ppermute | solution.py:28
  31.0 6.2 %collective-permute-start.12 = (f32[128,1,128]{2,0,1:T(8,128)S(1)}, f32[128,1,128]{2,0,1:T(8,128)S(1)}, u32[]{:S(2)}, u32[]{:S(2)}) collective-permute-start(f32[128,1,128]{2,0,1:T(8,128)S(1)} %bitcast.426), channel_id=1, source_target_pairs={{0,13},{1,14},{2,15},{3,0},{4,1},{5,2},{6,3},{7,4},{8,5},{9,6},{10... | collective-permute-start | bytes 196616 | tf_op jit(solution)/shard_map/ppermute | solution.py:28
  33.3 6.1 %collective-permute-start.13 = (f32[128,1,128]{2,0,1:T(8,128)S(1)}, f32[128,1,128]{2,0,1:T(8,128)S(1)}, u32[]{:S(2)}, u32[]{:S(2)}) collective-permute-start(f32[128,1,128]{2,0,1:T(8,128)S(1)} %bitcast.425), channel_id=1, source_target_pairs={{0,14},{1,15},{2,0},{3,1},{4,2},{5,3},{6,4},{7,5},{8,6},{9,7},{10,... | collective-permute-start | bytes 196616 | tf_op jit(solution)/shard_map/ppermute | solution.py:28
  36.7 3.2 %collective-permute-start.14 = (f32[128,1,128]{2,0,1:T(8,128)S(1)}, f32[128,1,128]{2,0,1:T(8,128)S(1)}, u32[]{:S(2)}, u32[]{:S(2)}) collective-permute-start(f32[128,1,128]{2,0,1:T(8,128)S(1)} %bitcast.424), channel_id=1, source_target_pairs={{0,15},{1,0},{2,1},{3,2},{4,3},{5,4},{6,5},{7,6},{8,7},{9,8},{10,9... | collective-permute-start | bytes 196616 | tf_op jit(solution)/shard_map/ppermute | solution.py:28
